TPU v7x, 32 devices: a whole 2x2x4 slice. The times are simulated.
32 devices in a mesh: dp: 8 (over y, x, core), tensor: 4 (over z).
Axes of the slice: x: 2, y: 2, z: 4, core: 2. Of those that a mesh axis runs over, the one named last changes fastest.
Arguments:
- tokens: bfloat16 [20480, 768], P(('dp', 'tensor')), may hold values from -6 to 6
- visible_counts: int32 [256], P('dp'), may hold values from 20 to 78, as said below
- norm_one_gain: float32 [768], replicated, may hold values from 0.1 to 1.9
- norm_one_shift: float32 [768], replicated, may hold values from -1.8 to 1.8
- input_weight: bfloat16 [768, 3, 768], P(None, None, 'tensor'), may hold values from -0.21875 to 0.21875
- input_bias: bfloat16 [2, 768], P(None, 'tensor'), may hold values from -1.796875 to 1.796875
- mixer_weight: bfloat16 [768, 768], P('tensor'), may hold values from -1.25 to 1.25
- mixer_bias: float32 [768], replicated, may hold values from -1.8 to 1.8
- norm_two_gain: float32 [768], replicated, may hold values from 0.1 to 1.9
- norm_two_shift: float32 [768], replicated, may hold values from -1.8 to 1.8
- up_weight: bfloat16 [768, 3072], P(None, 'tensor'), may hold values from -0.21875 to 0.21875
- up_bias: bfloat16 [3072], P('tensor'), may hold values from -1.796875 to 1.796875
- down_weight: bfloat16 [3072, 768], P('tensor'), may hold values from -0.109375 to 0.109375
- down_bias: float32 [768], replicated, may hold values from -1.8 to 1.8
- output_grad: bfloat16 [20480, 768], P(('dp', 'tensor')), may hold values from -6 to 6
Outputs:
- block_output: bfloat16 [20480, 768], P(('dp', 'tensor'))
- grad_tokens: float32 [20480, 768], P(('dp', 'tensor'))
- grad_norm_one_gain: float32 [768], replicated
- grad_norm_one_shift: float32 [768], replicated
- grad_input_weight: float32 [768, 3, 768], P(None, None, 'tensor')
- grad_input_bias: float32 [2, 768], P(None, 'tensor')
- grad_mixer_weight: float32 [768, 768], P('tensor')
- grad_mixer_bias: float32 [768], replicated
- grad_norm_two_gain: float32 [768], replicated
- grad_norm_two_shift: float32 [768], replicated
- grad_up_weight: float32 [768, 3072], P(None, 'tensor')
- grad_up_bias: float32 [3072], P('tensor')
- grad_down_weight: float32 [3072, 768], P('tensor')
- grad_down_bias: float32 [768], replicated
Inputs may be any that keep to these rules, and one draw needn't show every extreme that they name: `visible_counts`: each image has 20 to 78 visible patches; some image has exactly 78 and some exactly 20.
All inputs are finite; a program needn't handle non-finite values.
Results may differ from a plain program's by a relative error of at most 0.014.
Values may be sent and summed in bfloat16 or wider, within the bound.
No kernel may reach another device: no remote copies, remote signals or barrier semaphores. Data moves between devices by JAX's collectives and lax.ppermute only.
A program may use at most 128 MiB of HBM per device.

v0:
```python
import jax
import jax.numpy as jnp
from jax import lax
from jax.sharding import PartitionSpec as P

HD = 64
SLOTS = 80
masked_score = -1000000000.0


def layer_norm(inputs, norm_gain, norm_shift):
    center = inputs - jnp.mean(inputs, axis=-1, keepdims=True)
    spread = jnp.mean(center * center, axis=-1, keepdims=True)
    return center * lax.rsqrt(spread + 1e-06) * norm_gain + norm_shift


def norm_back(inputs, norm_gain, norm_shift, grad_normed):
    unused, pullback = jax.vjp(layer_norm, inputs, norm_gain, norm_shift)
    return pullback(grad_normed)


def gelu_exact(inputs):
    return jax.nn.gelu(inputs, approximate=False)


def split_heads(flat, slot_count, head_dim):
    return flat.reshape(
        flat.shape[0] // slot_count, slot_count, flat.shape[1] // head_dim, head_dim
    )


def visible_keys(counts, slot_count):
    return (lax.broadcasted_iota(jnp.int32, (counts.shape[0], slot_count), 1) < counts[:, None])[
        :, None, None, :
    ]


def project_inputs(normed_rows, weight_in, bias_in, slot_count, head_dim):
    columns = weight_in.shape[2]
    product = jnp.dot(
        normed_rows,
        weight_in.reshape(weight_in.shape[0], 3 * columns),
        preferred_element_type=jnp.float32,
    ).reshape(-1, 3, columns)
    queries = (product[:, 0] + bias_in[0]).astype(jnp.bfloat16)
    key_rows = product[:, 1].astype(jnp.bfloat16)
    values = (product[:, 2] + bias_in[1]).astype(jnp.bfloat16)
    return (
        split_heads(queries, slot_count, head_dim),
        split_heads(key_rows, slot_count, head_dim),
        split_heads(values, slot_count, head_dim),
    )


def attend(queries, key_rows, values, counts):
    factor = queries.shape[-1] ** (-0.5)
    scores = (
        jnp.einsum("bqhd,bkhd->bhqk", queries, key_rows, preferred_element_type=jnp.float32)
        * factor
    )
    scores = jnp.where(visible_keys(counts, key_rows.shape[1]), scores, masked_score)
    maxima = jnp.max(scores, axis=-1, keepdims=True)
    exponent = jnp.exp(scores - maxima)
    totals = jnp.sum(exponent, axis=-1, keepdims=True)
    soft_low = (exponent / totals).astype(jnp.bfloat16)
    blended = jnp.einsum("bhqk,bkhd->bqhd", soft_low, values, preferred_element_type=jnp.float32)
    return (blended, maxima + jnp.log(totals))


def attend_back(queries, key_rows, values, counts, log_totals, grad_blend):
    factor = queries.shape[-1] ** (-0.5)
    scores = (
        jnp.einsum("bqhd,bkhd->bhqk", queries, key_rows, preferred_element_type=jnp.float32)
        * factor
    )
    scores = jnp.where(visible_keys(counts, key_rows.shape[1]), scores, masked_score)
    soft = jnp.exp(scores - log_totals)
    soft_low = soft.astype(jnp.bfloat16)
    grad_values = jnp.einsum(
        "bhqk,bqhd->bkhd", soft_low, grad_blend, preferred_element_type=jnp.float32
    )
    grad_soft = jnp.einsum(
        "bqhd,bkhd->bhqk", grad_blend, values, preferred_element_type=jnp.float32
    )
    grad_scores = soft * (grad_soft - jnp.sum(grad_soft * soft, axis=-1, keepdims=True))
    grad_low = grad_scores.astype(jnp.bfloat16)
    grad_queries = (
        jnp.einsum("bhqk,bkhd->bqhd", grad_low, key_rows, preferred_element_type=jnp.float32)
        * factor
    )
    grad_keys = (
        jnp.einsum("bhqk,bqhd->bkhd", grad_low, queries, preferred_element_type=jnp.float32)
        * factor
    )
    return (grad_queries, grad_keys, grad_values)


def mlp_back(normed_rows, hidden_pre, active, grad_rows, weight_down):
    grad_down = jnp.einsum("rf,rd->fd", active, grad_rows, preferred_element_type=jnp.float32)
    grad_active = jnp.einsum(
        "rd,fd->rf", grad_rows, weight_down, preferred_element_type=jnp.float32
    )
    unused, pullback = jax.vjp(gelu_exact, hidden_pre)
    grad_pre = pullback(grad_active)[0]
    grad_up_b = jnp.sum(grad_pre, axis=0)
    grad_pre_low = grad_pre.astype(jnp.bfloat16)
    grad_up = jnp.einsum("rd,rf->df", normed_rows, grad_pre_low, preferred_element_type=jnp.float32)
    return (grad_down, grad_up, grad_up_b, grad_pre_low)


def mixer_back(
    normed_rows,
    queries,
    key_rows,
    values,
    counts,
    log_totals,
    grad_rows,
    blend_low,
    weight_mix,
    slot_count,
    head_dim,
):
    row_total = blend_low.shape[0]
    grad_mix = jnp.einsum("rc,rd->cd", blend_low, grad_rows, preferred_element_type=jnp.float32)
    grad_blend = jnp.einsum(
        "rd,cd->rc", grad_rows, weight_mix, preferred_element_type=jnp.float32
    ).astype(jnp.bfloat16)
    grad_queries, grad_keys, grad_values = attend_back(
        queries, key_rows, values, counts, log_totals, split_heads(grad_blend, slot_count, head_dim)
    )
    grad_queries = grad_queries.reshape(row_total, -1)
    grad_keys = grad_keys.reshape(row_total, -1)
    grad_values = grad_values.reshape(row_total, -1)
    grad_bias_in = jnp.stack([jnp.sum(grad_queries, axis=0), jnp.sum(grad_values, axis=0)])
    grad_projected = jnp.stack([grad_queries, grad_keys, grad_values], axis=1).astype(jnp.bfloat16)
    grad_weight_in = jnp.einsum(
        "rd,rjc->djc", normed_rows, grad_projected, preferred_element_type=jnp.float32
    )
    return (grad_mix, grad_bias_in, grad_weight_in, grad_projected)


def local(
    tokens,
    visible_counts,
    norm_one_gain,
    norm_one_shift,
    input_weight,
    input_bias,
    mixer_weight,
    mixer_bias,
    norm_two_gain,
    norm_two_shift,
    up_weight,
    up_bias,
    down_weight,
    down_bias,
    output_grad,
):
    slot_count = SLOTS
    head_dim = HD
    inputs = tokens.astype(jnp.float32)
    grad_output = output_grad.astype(jnp.float32)
    low_one = layer_norm(inputs, norm_one_gain, norm_one_shift).astype(jnp.bfloat16)
    whole_one = lax.all_gather(low_one, "tensor", axis=0, tiled=True)
    queries, key_rows, values = project_inputs(
        whole_one, input_weight, input_bias, slot_count, head_dim
    )
    blended, log_totals = attend(queries, key_rows, values, visible_counts)
    blend_low = blended.reshape(whole_one.shape[0], -1).astype(jnp.bfloat16)
    first_sum = (
        inputs
        + lax.psum_scatter(
            jnp.dot(blend_low, mixer_weight, preferred_element_type=jnp.float32),
            "tensor",
            scatter_dimension=0,
            tiled=True,
        )
        + mixer_bias
    )
    low_two = layer_norm(first_sum, norm_two_gain, norm_two_shift).astype(jnp.bfloat16)
    whole_two = lax.all_gather(low_two, "tensor", axis=0, tiled=True)
    hidden_pre = jnp.dot(whole_two, up_weight, preferred_element_type=jnp.float32) + up_bias
    active = gelu_exact(hidden_pre).astype(jnp.bfloat16)
    result = (
        first_sum
        + lax.psum_scatter(
            jnp.dot(active, down_weight, preferred_element_type=jnp.float32).astype(jnp.bfloat16),
            "tensor",
            scatter_dimension=0,
            tiled=True,
        ).astype(jnp.float32)
        + down_bias
    )
    whole_grad = lax.all_gather(output_grad, "tensor", axis=0, tiled=True)
    grad_down, grad_up, grad_up_b, grad_pre_low = mlp_back(
        whole_two, hidden_pre, active, whole_grad, down_weight
    )
    grad_normed_two = lax.psum_scatter(
        jnp.einsum("rf,df->rd", grad_pre_low, up_weight, preferred_element_type=jnp.float32),
        "tensor",
        scatter_dimension=0,
        tiled=True,
    )
    grad_first, grad_gain_two, grad_shift_two = norm_back(
        first_sum, norm_two_gain, norm_two_shift, grad_normed_two
    )
    grad_first = grad_output + grad_first
    whole_first = lax.all_gather(grad_first.astype(jnp.bfloat16), "tensor", axis=0, tiled=True)
    grad_mix, grad_bias_in, grad_weight_in, grad_projected = mixer_back(
        whole_one,
        queries,
        key_rows,
        values,
        visible_counts,
        log_totals,
        whole_first,
        blend_low,
        mixer_weight,
        slot_count,
        head_dim,
    )
    grad_normed_one = lax.psum_scatter(
        jnp.einsum(
            "rjc,djc->rd", grad_projected, input_weight, preferred_element_type=jnp.float32
        ).astype(jnp.bfloat16),
        "tensor",
        scatter_dimension=0,
        tiled=True,
    ).astype(jnp.float32)
    weight_terms = (grad_weight_in, grad_bias_in, grad_mix, grad_up, grad_up_b, grad_down)
    grad_inputs, grad_gain_one, grad_shift_one = norm_back(
        inputs, norm_one_gain, norm_one_shift, grad_normed_one
    )
    grad_tokens = grad_first + grad_inputs
    sum_gain_one, sum_shift_one, sum_mix_bias, sum_gain_two, sum_shift_two, sum_down_bias = (
        lax.psum(
            (
                grad_gain_one,
                grad_shift_one,
                jnp.sum(grad_first, axis=0),
                grad_gain_two,
                grad_shift_two,
                jnp.sum(grad_output, axis=0),
            ),
            ("dp", "tensor"),
        )
    )
    sum_weight_in, sum_bias_in, sum_mix, sum_up, sum_up_b, sum_down = lax.psum(
        (
            weight_terms[0],
            weight_terms[1],
            weight_terms[2],
            weight_terms[3],
            weight_terms[4],
            weight_terms[5],
        ),
        "dp",
    )
    return (
        result.astype(jnp.bfloat16),
        grad_tokens,
        sum_gain_one,
        sum_shift_one,
        sum_weight_in,
        sum_bias_in,
        sum_mix,
        sum_mix_bias,
        sum_gain_two,
        sum_shift_two,
        sum_up,
        sum_up_b,
        sum_down,
        sum_down_bias,
    )


def solution(mesh):
    in_specs = (
        P(("dp", "tensor"), None),
        P("dp"),
        P(),
        P(),
        P(None, None, "tensor"),
        P(None, "tensor"),
        P("tensor", None),
        P(),
        P(),
        P(),
        P(None, "tensor"),
        P("tensor"),
        P("tensor", None),
        P(),
        P(("dp", "tensor"), None),
    )
    out_specs = (
        P(("dp", "tensor"), None),
        P(("dp", "tensor"), None),
        P(),
        P(),
        P(None, None, "tensor"),
        P(None, "tensor"),
        P("tensor", None),
        P(),
        P(),
        P(),
        P(None, "tensor"),
        P("tensor"),
        P("tensor", None),
        P(),
    )
    return jax.shard_map(local, mesh=mesh, in_specs=in_specs, out_specs=out_specs, check_vma=False)
```

profile of v0, /device:TPU:0, one launch (start us, length us, event | category | flops | bytes accessed | tf_op | source)
XLA Modules:
  0.0 1010.1 jit_solution(16693348201039939642)
XLA Ops:
  7.3 1.5 convert_reduce_fusion.1
  8.8 1.6 fusion.20
  11.7 2.6 fusion.19
  14.6 79.0 %all-gather.5.cloned.1.call-done = bf16[2560,768]{1,0:T(8,128)(2,1)} async-done(((bf16[640,768]{1,0:T(8,128)(2,1)}), bf16[2560,768]{1,0:T(8,128)(2,1)}) %all-gather.5.cloned.1.call-update) | async-done | bytes 3932176 | tf_op jit(solution)/shard_map/all_gather | solution.py:165
  93.6 4.6 fusion.6
  99.2 2.2 fusion.56
  101.4 3.3 convert_element_type.82
  104.7 4.7 squeeze.4
  109.4 4.1 squeeze.10
  113.5 5.2 fusion.57
  119.9 2.2 copy-done.9
  122.1 3.0 fusion.34
  125.1 2.2 copy.43
  127.2 3.6 convert_element_type.86
  130.9 4.3 fusion.58
  135.3 134.9 %reduce-scatter.5.cloned.1.call-done = f32[640,768]{1,0:T(8,128)} async-done(((f32[2560,768]{1,0:T(8,128)}), f32[640,768]{1,0:T(8,128)}) %reduce-scatter.5.cloned.1.call-update) | async-done | bytes 1966096 | tf_op jit(solution)/shard_map/reduce_scatter | solution.py:173
  270.2 2.1 fusion.54
  272.7 1.3 add_convert_fusion.1
  274.7 76.5 %all-gather.7.cloned.1.call-done = bf16[2560,768]{1,0:T(8,128)(2,1)} async-done(((bf16[640,768]{1,0:T(8,128)(2,1)}), bf16[2560,768]{1,0:T(8,128)(2,1)}) %all-gather.7.cloned.1.call-update) | async-done | bytes 3932176 | tf_op jit(solution)/shard_map/all_gather | solution.py:182
  351.2 9.0 fusion.59
  360.2 67.5 %all-gather.9.cloned.1.call-done = bf16[2560,768]{1,0:T(8,128)(2,1)} async-done(((bf16[640,768]{1,0:T(8,128)(2,1)}), bf16[2560,768]{1,0:T(8,128)(2,1)}) %all-gather.9.cloned.1.call-update) | async-done | bytes 3932176 | tf_op jit(solution)/shard_map/all_gather | solution.py:195
  427.6 23.8 %fusion.51 = (f32[768]{0:T(1024)S(1)}, bf16[2560,768]{1,0:T(8,128)(2,1)S(1)}, f32[2560,768]{1,0:T(8,128)}) fusion(f32[2560,768]{1,0:T(8,128)} %fusion.59, f32[768]{0:T(1024)S(1)} %convert_element_type.88, bf16[2560,768]{1,0:T(8,128)(2,1)} %all-gather.9.cloned.1.call-done, bf16[768,768]{1,0:T(8,128)(2,1)S(1)} %copy-done), kind=kOutput, calls=%fused_computation.106 | convolution fusion | flops 3165388032 | bytes 24778752 | tf_op jit(solution)/shard_map/rd,fd->rf/dot_general | solution.py:100
  451.4 1.9 copy-done.46
  453.3 5.4 fusion.29
  459.2 8.0 multiply_convert_fusion
  467.2 2.0 copy-done.15
  469.2 4.7 convolution_convert_fusion
  473.9 119.7 %reduce-scatter.9.cloned.1.call-done = f32[640,768]{1,0:T(8,128)} async-done(((f32[2560,768]{1,0:T(8,128)}), f32[640,768]{1,0:T(8,128)}) %reduce-scatter.9.cloned.1.call-update) | async-done | bytes 1966096 | tf_op jit(solution)/shard_map/reduce_scatter | solution.py:199
  593.7 2.3 multiply_reduce_fusion.1
  596.0 73.1 %reduce-scatter.7.cloned.1.call-done = bf16[640,768]{1,0:T(8,128)(2,1)} async-done(((bf16[2560,768]{1,0:T(8,128)(2,1)}), bf16[640,768]{1,0:T(8,128)(2,1)}) %reduce-scatter.7.cloned.1.call-update) | async-done | bytes 983056 | tf_op jit(solution)/shard_map/reduce_scatter | solution.py:187
  669.0 3.7 fusion.53
  672.7 1.3 copy-done.5
  675.4 76.9 %all-gather.11.cloned.1.call-done = bf16[2560,768]{1,0:T(8,128)(2,1)} async-done(((bf16[640,768]{1,0:T(8,128)(2,1)}), bf16[2560,768]{1,0:T(8,128)(2,1)}) %all-gather.11.cloned.1.call-update) | async-done | bytes 3932176 | tf_op jit(solution)/shard_map/all_gather | solution.py:209
  752.2 4.5 convolution_convert_fusion.1
  756.7 3.3 reshape.157
  760.0 7.1 multiply_reduce_fusion
  767.1 3.0 bitcast_convert_fusion.1
  772.0 4.0 fusion.33
  776.1 3.4 bitcast_convert_fusion.2
  780.6 3.9 stack_reshape.14
  784.4 2.4 copy.49
  786.9 3.7 stack_reshape.13
  790.5 2.4 copy.47
  793.0 3.7 stack_reshape.12
  796.6 1.4 constant_dynamic-update-slice_fusion.2
  798.0 1.3 constant_dynamic-update-slice_fusion.1
  799.4 1.6 copy-done.22
  800.9 4.7 bitcast_convert_fusion
  806.0 8.1 fusion.27
  814.2 4.8 fusion.61
  819.1 1.7 fusion.60
  820.9 3.7 fusion.62
  824.6 2.3 bitcast_reduce_fusion
  827.0 2.4 bitcast_reduce_fusion.1
  829.5 14.4 %all-reduce.1 = (f32[2,192]{1,0:T(2,128)}, f32[768]{0:T(1024)}) all-reduce(f32[2,192]{1,0:T(2,128)S(1)} %pad_maximum_fusion, f32[768]{0:T(1024)S(1)} %get-tuple-element.37), channel_id=1, replica_groups=mesh['dp'=8,'tensor'=4] {'dp'}, use_global_device_ids=true, to_apply=%region_22.23 | all-reduce | flops 1152 | bytes 9216 | tf_op jit(solution)/shard_map/psum | solution.py:249
  843.9 33.2 %reduce-scatter.11.cloned.1.call-done = bf16[640,768]{1,0:T(8,128)(2,1)} async-done(((bf16[2560,768]{1,0:T(8,128)(2,1)}), bf16[640,768]{1,0:T(8,128)(2,1)}) %reduce-scatter.11.cloned.1.call-update) | async-done | bytes 983056 | tf_op jit(solution)/shard_map/reduce_scatter | solution.py:223
  877.1 2.0 convert_reduce_fusion
  879.2 2.3 fusion.23
  881.6 2.2 convert_reduce_fusion.2
  883.8 41.7 %all-reduce = (f32[768]{0:T(1024)}, f32[768]{0:T(1024)}, f32[768]{0:T(1024)}, f32[768]{0:T(1024)}, f32[768]{0:T(1024)}, /*index=5*/f32[768]{0:T(1024)}) all-reduce(f32[768]{0:T(1024)S(1)} %get-tuple-element.16, f32[768]{0:T(1024)S(1)} %get-tuple-element.21, ...), channel_id=1, replica_groups=mesh['dp'=8,'tensor'=4] {'dp','tensor'}, use_global_device_ids=true, to_apply=%region_16.17 | all-reduce | flops 4608 | bytes 36864 | tf_op jit(solution)/shard_map/psum | solution.py:237
  925.4 71.1 %all-reduce.5.cloned.1.call-done = (f32[768,3,192]{0,2,1:T(8,128)}, f32[192,768]{1,0:T(8,128)}, f32[768,768]{1,0:T(8,128)}, f32[768,768]{1,0:T(8,128)}) async-done(((f32[768,3,192]{0,2,1:T(8,128)}, f32[192,768]{1,0:T(8,128)}, f32[768,768]{1,0:T(8,128)}, f32[768,768]{1,0:T(8,128)}), (f32[768,3,192]{0,2,1:T(8,128)}, f32[192,768]{1,0:T(8,128)}, f32[768,768]{1,0:T(8,128)}, ...) | async-done | bytes 7077904 | tf_op jit(solution)/shard_map/psum | solution.py:249
  996.5 2.9 copy.93
  1000.3 1.4 copy.95
  1001.7 1.4 copy.96
  (132 shorter events, 11.3 us)
Async XLA Ops:
  7.2 420.5 %copy-start = (bf16[768,768]{1,0:T(8,128)(2,1)S(1)}, bf16[768,768]{1,0:T(8,128)(2,1)}, u32[]{:S(2)}) copy-start(bf16[768,768]{1,0:T(8,128)(2,1)} %param.27) | copy-start | bytes 3538948
  7.2 7.1 copy-start.38
  7.2 7.3 copy-start.40
  7.2 86.3 %copy-start.44 = (bf16[768,3,192]{0,2,1:T(8,128)(2,1)S(1)}, bf16[768,3,192]{0,2,1:T(8,128)(2,1)}, u32[]{:S(2)}) copy-start(bf16[768,3,192]{0,2,1:T(8,128)(2,1)} %param.19) | copy-start | bytes 2654212
  7.2 86.3 %all-gather.5.cloned.1.call-start = ((), (), s32[]{:S(2)}) async-start(), calls=%async_computation.4 | async-start | bytes 4915200 | tf_op jit(solution)/shard_map/all_gather | solution.py:165
  8.8 2.2 copy-start.27
  10.4 0.6 copy-start.32
  11.1 0.6 copy-start.30
  14.3 255.9 %reduce-scatter.5.cloned.1.call-start = ((), (), s32[]{:S(2)}) async-start(), calls=%async_computation.5 | async-start | bytes 9830400 | tf_op jit(solution)/shard_map/reduce_scatter | solution.py:173
  104.7 8.9 copy-start.7
  118.7 6.3 copy-start.1
  118.8 3.3 copy-start.9
  122.1 3.0 copy-start.25
  125.1 5.8 copy-start.24
  130.9 4.3 copy-start.10
  135.2 135.0 %copy-start.35 = (f32[768]{0:T(1024)S(1)}, f32[768]{0:T(1024)}, u32[]{:S(2)}) copy-start(f32[768]{0:T(1024)} %param.22) | copy-start | bytes 9220
  135.2 137.5 %copy-start.34 = (f32[768]{0:T(1024)S(1)}, f32[768]{0:T(1024)}, u32[]{:S(2)}) copy-start(f32[768]{0:T(1024)} %param.23) | copy-start | bytes 9220
  135.2 137.5 %copy-start.36 = (f32[768]{0:T(1024)S(1)}, f32[768]{0:T(1024)}, u32[]{:S(2)}) copy-start(f32[768]{0:T(1024)} %param.24) | copy-start | bytes 9220
  135.3 215.9 %all-gather.7.cloned.1.call-start = ((), (), s32[]{:S(2)}) async-start(), calls=%async_computation.6 | async-start | bytes 4915200 | tf_op jit(solution)/shard_map/all_gather | solution.py:182
  272.3 2.4 copy-start.39
  274.1 153.6 %all-gather.9.cloned.1.call-start = ((), (), s32[]{:S(2)}) async-start(), calls=%async_computation.8 | async-start | bytes 4915200 | tf_op jit(solution)/shard_map/all_gather | solution.py:195
  274.6 319.0 %reduce-scatter.9.cloned.1.call-start = ((), (), s32[]{:S(2)}) async-start(), calls=%async_computation.9 | async-start | bytes 9830400 | tf_op jit(solution)/shard_map/reduce_scatter | solution.py:199
  427.6 25.7 %copy-start.43 = (bf16[768,768]{1,0:T(8,128)(2,1)S(1)}, bf16[768,768]{1,0:T(8,128)(2,1)}, u32[]{:S(2)}) copy-start(bf16[768,768]{1,0:T(8,128)(2,1)} %param.25) | copy-start | bytes 3538948
  451.4 1.9 copy-start.46
  458.7 210.3 %reduce-scatter.7.cloned.1.call-start = ((), (), s32[]{:S(2)}) async-start(), calls=%async_computation.7 | async-start | bytes 4915200 | tf_op jit(solution)/shard_map/reduce_scatter | solution.py:187
  467.2 2.0 copy-start.15
  473.8 195.2 %copy-start.37 = (f32[768]{0:T(1024)S(1)}, f32[768]{0:T(1024)}, u32[]{:S(2)}) copy-start(f32[768]{0:T(1024)} %param.28) | copy-start | bytes 9220
  473.9 278.3 %all-gather.11.cloned.1.call-start = ((), (), s32[]{:S(2)}) async-start(), calls=%async_computation.10 | async-start | bytes 4915200 | tf_op jit(solution)/shard_map/all_gather | solution.py:209
  669.0 5.0 copy-start.12
  672.7 1.3 copy-start.5
  672.7 2.6 copy-start.26
  675.3 201.8 %reduce-scatter.11.cloned.1.call-start = ((), (), s32[]{:S(2)}) async-start(), calls=%async_computation.11 | async-start | bytes 4915200 | tf_op jit(solution)/shard_map/reduce_scatter | solution.py:223
  759.9 7.2 copy-start.2
  770.2 1.9 copy-start.4
  772.0 4.0 copy-start.8
  796.6 2.7 copy-start.18
  796.6 4.3 copy-start.45
  799.4 1.6 copy-start.22
  805.7 190.8 %all-reduce.5.cloned.1.call-start = ((), (), s32[]{:S(2)}) async-start(), calls=%async_computation.12 | async-start | bytes 14155776 | tf_op jit(solution)/shard_map/psum | solution.py:249
  806.0 8.2 copy-start.16
  806.0 8.2 copy-start.42
  814.2 4.9 copy-start.11
  814.2 4.9 copy-start.17
  814.2 6.6 copy-start.41
  819.1 1.9 copy-start.23
  824.6 52.5 %copy-start.3 = (bf16[640,768]{1,0:T(8,128)(2,1)S(1)}, bf16[640,768]{1,0:T(8,128)(2,1)}, u32[]{:S(2)}) copy-start(bf16[640,768]{1,0:T(8,128)(2,1)} %param.15) | copy-start | bytes 2949124
  824.6 52.5 %copy-start.28 = (f32[640]{0:T(1024)S(1)}, f32[640]{0:T(1024)}, u32[]{:S(2)}) copy-start(f32[640]{0:T(1024)} %copy-done.27) | copy-start | bytes 7684
  824.6 52.5 %copy-start.29 = (f32[768]{0:T(1024)S(1)}, f32[768]{0:T(1024)}, u32[]{:S(2)}) copy-start(f32[768]{0:T(1024)} %param.17) | copy-start | bytes 9220
  826.9 52.3 %copy-start.33 = (f32[640]{0:T(1024)S(1)}, f32[640]{0:T(1024)}, u32[]{:S(2)}) copy-start(f32[640]{0:T(1024)} %copy-done.32) | copy-start | bytes 7684
  826.9 52.3 %copy-start.31 = (f32[640]{0:T(1024)S(1)}, f32[640]{0:T(1024)}, u32[]{:S(2)}) copy-start(f32[640]{0:T(1024)} %copy-done.30) | copy-start | bytes 7684
  827.0 54.6 %copy-start.13 = (bf16[640,768]{1,0:T(8,128)(2,1)S(1)}, bf16[640,768]{1,0:T(8,128)(2,1)}, u32[]{:S(2)}) copy-start(bf16[640,768]{1,0:T(8,128)(2,1)} %param.29) | copy-start | bytes 2949124
  877.1 4.5 copy-start.6
  877.1 4.5 copy-start.14
  996.5 3.0 copy-start.21
  996.5 3.8 copy-start.20
  999.5 2.2 copy-start.19
Sparse Core Ops, SparseCore 0:
  14.4 79.1 all-gather.4
  135.4 134.8 reduce-scatter.4
  274.2 76.9 all-gather.6
  352.6 74.9 all-gather.8
  458.8 134.8 reduce-scatter.8
  595.8 73.1 reduce-scatter.6
  675.4 76.7 all-gather.10
  805.8 71.2 reduce-scatter.10
  881.9 114.5 all-reduce.4
where the time goes:
time: 1010 us
  waiting for transfers between devices  732 us (72%)
  matrix products  105 us (10%)
  local copies, waits for them, and re-layouts  62.3 us (6%)
  blocking collectives  56.1 us (6%)
  other arithmetic  38.2 us (4%)
  between operations  14.8 us (1%)
    reduce_scatter x1, waiting for transfers between devices, local(): lax.psum_scatter(jnp.dot(blend_low, mixer_weight, preferred_element_type=...  135 us
    reduce_scatter x1, waiting for transfers between devices, local(): lax.psum_scatter(jnp.einsum('rf,df->rd', grad_pre_low, up_weight, preferr...  120 us
    all_gather x1, waiting for transfers between devices, local(): whole_one = lax.all_gather(low_one, 'tensor', axis=0, tiled=True)  79 us
    all_gather x1, waiting for transfers between devices, local(): lax.all_gather(grad_first.astype(jnp.bfloat16), 'tensor', axis=0, tiled=T...  76.9 us
    all_gather x1, waiting for transfers between devices, local(): whole_two = lax.all_gather(low_two, 'tensor', axis=0, tiled=True)  76.5 us
    reduce_scatter x1, waiting for transfers between devices, local(): lax.psum_scatter(jnp.dot(active, down_weight, preferred_element_type=jnp....  73.1 us
    psum x1, waiting for transfers between devices, local(): lax.psum((weight_terms[0], weight_terms[1], weight_terms[2], weight_terms...  71.1 us
    all_gather x1, waiting for transfers between devices, local(): whole_grad = lax.all_gather(output_grad, 'tensor', axis=0, tiled=True)  67.5 us
  transfers between devices with their start and end apart: 9, of which 9 were waited for; matrix products, arithmetic and copies ran while one was open for 5% of the time, Pallas kernels for 0%

commit v1 on v0

--- a/solution.py
+++ b/solution.py
@@ -6,6 +6,19 @@
 HD = 64
 SLOTS = 80
 masked_score = -1000000000.0
+
+
+def gather_around(x, axis, dim):
+    devices, place, extent = (lax.axis_size(axis), lax.axis_index(axis), x.shape[dim])
+    ahead = [(i, (i + 1) % devices) for i in range(devices)]
+    out = jnp.zeros((*x.shape[:dim], devices * extent, *x.shape[dim + 1 :]), x.dtype)
+    held = x
+    for step in range(devices):
+        source = (place - step) % devices
+        out = lax.dynamic_update_slice_in_dim(out, held, source * extent, axis=dim)
+        if step < devices - 1:
+            held = lax.ppermute(held, axis, ahead)
+    return out
 
 
 def layer_norm(inputs, norm_gain, norm_shift):
@@ -162,7 +175,7 @@
     inputs = tokens.astype(jnp.float32)
     grad_output = output_grad.astype(jnp.float32)
     low_one = layer_norm(inputs, norm_one_gain, norm_one_shift).astype(jnp.bfloat16)
-    whole_one = lax.all_gather(low_one, "tensor", axis=0, tiled=True)
+    whole_one = gather_around(low_one, "tensor", 0)
     queries, key_rows, values = project_inputs(
         whole_one, input_weight, input_bias, slot_count, head_dim
     )

time: 1010 us -> 1010 us (level)
    all_gather x1 -> x0, waiting for transfers between devices: 79 us -> none  [local(): whole_one = lax.all_gather(low_one, 'tensor', axis=0, tiled=True)]
    ppermute x0 -> x3, waiting for transfers between devices: none -> 70.1 us  [gather_around(): held = lax.ppermute(held, axis, ahead)]
    unnamed x100 -> x108, local copies, waits for them, and re-layouts: 20.5 us -> 22.3 us
  transfers between devices with their start and end apart: 9 -> 11, of which waited for: 9 -> 11; matrix products, arithmetic and copies ran while one was open for 5% -> 6% of each run, Pallas kernels for 0% -> 0%
where the time goes in v1:
time: 1010 us
  waiting for transfers between devices  722 us (71%)
  matrix products  105 us (10%)
  local copies, waits for them, and re-layouts  68.7 us (7%)
  blocking collectives  56.1 us (6%)
  other arithmetic  36.1 us (4%)
  between operations  15.1 us (1%)
    reduce_scatter x1, waiting for transfers between devices, local(): lax.psum_scatter(jnp.dot(blend_low, mixer_weight, preferred_element_type=...  134 us
    reduce_scatter x1, waiting for transfers between devices, local(): lax.psum_scatter(jnp.einsum('rf,df->rd', grad_pre_low, up_weight, preferr...  120 us
    all_gather x1, waiting for transfers between devices, local(): lax.all_gather(grad_first.astype(jnp.bfloat16), 'tensor', axis=0, tiled=T...  76.9 us
    all_gather x1, waiting for transfers between devices, local(): whole_two = lax.all_gather(low_two, 'tensor', axis=0, tiled=True)  76.3 us
    reduce_scatter x1, waiting for transfers between devices, local(): lax.psum_scatter(jnp.dot(active, down_weight, preferred_element_type=jnp....  73 us
    psum x1, waiting for transfers between devices, local(): lax.psum((weight_terms[0], weight_terms[1], weight_terms[2], weight_terms...  71.1 us
    ppermute x3, waiting for transfers between devices, gather_around(): held = lax.ppermute(held, axis, ahead)  70.1 us
    all_gather x1, waiting for transfers between devices, local(): whole_grad = lax.all_gather(output_grad, 'tensor', axis=0, tiled=True)  67.6 us
  transfers between devices with their start and end apart: 11, of which 11 were waited for; matrix products, arithmetic and copies ran while one was open for 6% of the time, Pallas kernels for 0%

profile of v1, /device:TPU:0, one launch (start us, length us, event | category | flops | bytes accessed | tf_op | source)
XLA Modules:
  0.0 1007.5 jit_solution(4701065699389302121)
XLA Ops:
  7.3 1.5 convert_reduce_fusion.1
  8.8 1.6 fusion.20
  11.8 1.9 copy-done.19
  13.7 3.0 collective-permute-start
  16.7 23.8 %collective-permute-done = bf16[640,768]{1,0:T(8,128)(2,1)S(1)} collective-permute-done((bf16[640,768]{1,0:T(8,128)(2,1)S(1)}, bf16[640,768]{1,0:T(8,128)(2,1)S(1)}, u32[]{:S(2)}, u32[]{:S(2)}) %collective-permute-start) | collective-permute-done | bytes 983072 | tf_op jit(solution)/shard_map/ppermute | solution.py:20
  40.5 24.7 %collective-permute-done.1 = bf16[640,768]{1,0:T(8,128)(2,1)S(1)} collective-permute-done((bf16[640,768]{1,0:T(8,128)(2,1)S(1)}, bf16[640,768]{1,0:T(8,128)(2,1)S(1)}, u32[]{:S(2)}, u32[]{:S(2)}) %collective-permute-start.1) | collective-permute-done | bytes 983072 | tf_op jit(solution)/shard_map/ppermute | solution.py:20
  67.6 21.6 %collective-permute-done.2 = bf16[640,768]{1,0:T(8,128)(2,1)} collective-permute-done((bf16[640,768]{1,0:T(8,128)(2,1)S(1)}, bf16[640,768]{1,0:T(8,128)(2,1)}, u32[]{:S(2)}, u32[]{:S(2)}) %collective-permute-start.2) | collective-permute-done | bytes 983072 | tf_op jit(solution)/shard_map/ppermute | solution.py:20
  89.2 2.2 constant_dynamic-update-slice_fusion.3
  91.4 4.6 fusion.6
  97.1 2.2 fusion.57
  99.2 3.3 convert_element_type.82
  102.5 4.7 squeeze.4
  107.2 4.1 squeeze.10
  111.4 5.2 fusion.58
  117.7 2.2 copy-done.10
  119.9 3.0 fusion.34
  122.9 2.2 copy.43
  125.1 3.6 convert_element_type.86
  128.7 4.3 fusion.59
  133.1 134.1 %reduce-scatter.5.cloned.1.call-done = f32[640,768]{1,0:T(8,128)} async-done(((f32[2560,768]{1,0:T(8,128)}), f32[640,768]{1,0:T(8,128)}) %reduce-scatter.5.cloned.1.call-update) | async-done | bytes 1966096 | tf_op jit(solution)/shard_map/reduce_scatter | solution.py:186
  267.2 2.1 fusion.54
  271.9 76.3 %all-gather.4.cloned.1.call-done = bf16[2560,768]{1,0:T(8,128)(2,1)} async-done(((bf16[640,768]{1,0:T(8,128)(2,1)}), bf16[2560,768]{1,0:T(8,128)(2,1)}) %all-gather.4.cloned.1.call-update) | async-done | bytes 3932176 | tf_op jit(solution)/shard_map/all_gather | solution.py:195
  348.1 9.0 fusion.60
  357.1 67.6 %all-gather.6.cloned.1.call-done = bf16[2560,768]{1,0:T(8,128)(2,1)} async-done(((bf16[640,768]{1,0:T(8,128)(2,1)}), bf16[2560,768]{1,0:T(8,128)(2,1)}) %all-gather.6.cloned.1.call-update) | async-done | bytes 3932176 | tf_op jit(solution)/shard_map/all_gather | solution.py:208
  424.8 23.8 %fusion.51 = (f32[768]{0:T(1024)S(1)}, bf16[2560,768]{1,0:T(8,128)(2,1)S(1)}, f32[2560,768]{1,0:T(8,128)}) fusion(f32[2560,768]{1,0:T(8,128)} %fusion.60, f32[768]{0:T(1024)S(1)} %convert_element_type.88, bf16[2560,768]{1,0:T(8,128)(2,1)} %all-gather.6.cloned.1.call-done, bf16[768,768]{1,0:T(8,128)(2,1)S(1)} %copy-done), kind=kOutput, calls=%fused_computation.110 | convolution fusion | flops 3165388032 | bytes 24778752 | tf_op jit(solution)/shard_map/rd,fd->rf/dot_general | solution.py:113
  448.6 1.9 copy-done.50
  450.4 5.3 fusion.29
  456.3 8.0 multiply_convert_fusion
  464.3 2.0 copy-done.16
  466.2 4.7 convolution_convert_fusion
  471.0 119.8 %reduce-scatter.9.cloned.1.call-done = f32[640,768]{1,0:T(8,128)} async-done(((f32[2560,768]{1,0:T(8,128)}), f32[640,768]{1,0:T(8,128)}) %reduce-scatter.9.cloned.1.call-update) | async-done | bytes 1966096 | tf_op jit(solution)/shard_map/reduce_scatter | solution.py:212
  590.8 2.3 multiply_reduce_fusion.1
  593.1 73.0 %reduce-scatter.7.cloned.1.call-done = bf16[640,768]{1,0:T(8,128)(2,1)} async-done(((bf16[2560,768]{1,0:T(8,128)(2,1)}), bf16[640,768]{1,0:T(8,128)(2,1)}) %reduce-scatter.7.cloned.1.call-update) | async-done | bytes 983056 | tf_op jit(solution)/shard_map/reduce_scatter | solution.py:200
  666.1 3.7 fusion.53
  672.4 76.9 %all-gather.8.cloned.1.call-done = bf16[2560,768]{1,0:T(8,128)(2,1)} async-done(((bf16[640,768]{1,0:T(8,128)(2,1)}), bf16[2560,768]{1,0:T(8,128)(2,1)}) %all-gather.8.cloned.1.call-update) | async-done | bytes 3932176 | tf_op jit(solution)/shard_map/all_gather | solution.py:222
  749.3 4.5 convolution_convert_fusion.1
  753.8 3.3 reshape.157
  757.0 7.1 multiply_reduce_fusion
  764.2 3.0 bitcast_convert_fusion.1
  769.1 4.0 fusion.33
  773.2 3.4 bitcast_convert_fusion.2
  777.6 3.9 stack_reshape.14
  781.5 2.4 copy.49
  783.9 3.7 stack_reshape.13
  787.6 2.4 copy.47
  790.0 3.7 stack_reshape.12
  796.5 1.6 copy-done.25
  798.0 4.8 bitcast_convert_fusion
  803.1 8.1 fusion.27
  811.3 4.8 fusion.62
  816.1 1.7 fusion.61
  818.5 3.7 fusion.63
  822.2 2.3 bitcast_reduce_fusion
  824.6 2.4 bitcast_reduce_fusion.1
  827.1 14.4 %all-reduce.1 = (f32[2,192]{1,0:T(2,128)}, f32[768]{0:T(1024)}) all-reduce(f32[2,192]{1,0:T(2,128)S(1)} %pad_maximum_fusion, f32[768]{0:T(1024)S(1)} %get-tuple-element.37), channel_id=1, replica_groups=mesh['dp'=8,'tensor'=4] {'dp'}, use_global_device_ids=true, to_apply=%region_22.23 | all-reduce | flops 1152 | bytes 9216 | tf_op jit(solution)/shard_map/psum | solution.py:262
  841.5 32.7 %reduce-scatter.11.cloned.1.call-done = bf16[640,768]{1,0:T(8,128)(2,1)} async-done(((bf16[2560,768]{1,0:T(8,128)(2,1)}), bf16[640,768]{1,0:T(8,128)(2,1)}) %reduce-scatter.11.cloned.1.call-update) | async-done | bytes 983056 | tf_op jit(solution)/shard_map/reduce_scatter | solution.py:236
  874.2 2.0 convert_reduce_fusion
  876.3 2.3 fusion.23
  878.7 2.2 convert_reduce_fusion.2
  880.9 41.7 %all-reduce = (f32[768]{0:T(1024)}, f32[768]{0:T(1024)}, f32[768]{0:T(1024)}, f32[768]{0:T(1024)}, f32[768]{0:T(1024)}, /*index=5*/f32[768]{0:T(1024)}) all-reduce(f32[768]{0:T(1024)S(1)} %get-tuple-element.16, f32[768]{0:T(1024)S(1)} %get-tuple-element.21, ...), channel_id=1, replica_groups=mesh['dp'=8,'tensor'=4] {'dp','tensor'}, use_global_device_ids=true, to_apply=%region_16.17 | all-reduce | flops 4608 | bytes 36864 | tf_op jit(solution)/shard_map/psum | solution.py:250
  922.5 71.1 %all-reduce.5.cloned.1.call-done = (f32[768,3,192]{0,2,1:T(8,128)}, f32[192,768]{1,0:T(8,128)}, f32[768,768]{1,0:T(8,128)}, f32[768,768]{1,0:T(8,128)}) async-done(((f32[768,3,192]{0,2,1:T(8,128)}, f32[192,768]{1,0:T(8,128)}, f32[768,768]{1,0:T(8,128)}, f32[768,768]{1,0:T(8,128)}), (f32[768,3,192]{0,2,1:T(8,128)}, f32[192,768]{1,0:T(8,128)}, f32[768,768]{1,0:T(8,128)}, ...) | async-done | bytes 7077904 | tf_op jit(solution)/shard_map/psum | solution.py:262
  993.6 2.9 copy.97
  997.4 1.4 copy.99
  998.8 1.4 copy.100
  (147 shorter events, 19.3 us)
Async XLA Ops:
  7.2 417.6 %copy-start = (bf16[768,768]{1,0:T(8,128)(2,1)S(1)}, bf16[768,768]{1,0:T(8,128)(2,1)}, u32[]{:S(2)}) copy-start(bf16[768,768]{1,0:T(8,128)(2,1)} %param.27) | copy-start | bytes 3538948
  7.2 4.2 copy-start.3
  7.2 4.2 copy-start.32
  7.2 4.2 copy-start.39
  7.2 260.0 %reduce-scatter.5.cloned.1.call-start = ((), (), s32[]{:S(2)}) async-start(), calls=%async_computation.4 | async-start | bytes 9830400 | tf_op jit(solution)/shard_map/reduce_scatter | solution.py:186
  8.8 3.0 copy-start.30
  10.5 0.6 copy-start.36
  11.1 0.8 copy-start.34
  11.1 54.2 %copy-start.43 = (bf16[2,192]{1,0:T(2,128)(2,1)S(1)}, bf16[2,192]{1,0:T(2,128)(2,1)}, u32[]{:S(2)}) copy-start(bf16[2,192]{1,0:T(2,128)(2,1)} %param.20) | copy-start | bytes 2308
  11.1 54.4 %copy-start.45 = (s32[32]{0:T(128)S(1)}, s32[32]{0:T(128)}, u32[]{:S(2)}) copy-start(s32[32]{0:T(128)} %param.16) | copy-start | bytes 388
  11.8 1.9 copy-start.19
  13.7 26.8 %collective-permute-start = (bf16[640,768]{1,0:T(8,128)(2,1)S(1)}, bf16[640,768]{1,0:T(8,128)(2,1)S(1)}, u32[]{:S(2)}, u32[]{:S(2)}) collective-permute-start(bf16[640,768]{1,0:T(8,128)(2,1)S(1)} %get-tuple-element.45), channel_id=1, source_target_pairs={{0,1},{1,2},{2,3},{3,0},{4,5},{5,6},{6,7},{7,4},{8,9},{9,10},{10,1... | collective-permute-start | bytes 2949128 | tf_op jit(solution)/shard_map/ppermute | solution.py:20
  40.5 24.7 %collective-permute-start.1 = (bf16[640,768]{1,0:T(8,128)(2,1)S(1)}, bf16[640,768]{1,0:T(8,128)(2,1)S(1)}, u32[]{:S(2)}, u32[]{:S(2)}) collective-permute-start(bf16[640,768]{1,0:T(8,128)(2,1)S(1)} %collective-permute-done), channel_id=1, source_target_pairs={{0,1},{1,2},{2,3},{3,0},{4,5},{5,6},{6,7},{7,4},{8,9},{9,10},{10,1... | collective-permute-start | bytes 2949128 | tf_op jit(solution)/shard_map/ppermute | solution.py:20
  65.3 23.9 %collective-permute-start.2 = (bf16[640,768]{1,0:T(8,128)(2,1)S(1)}, bf16[640,768]{1,0:T(8,128)(2,1)}, u32[]{:S(2)}, u32[]{:S(2)}) collective-permute-start(bf16[640,768]{1,0:T(8,128)(2,1)S(1)} %collective-permute-done.1), channel_id=1, source_target_pairs={{0,1},{1,2},{2,3},{3,0},{4,5},{5,6},{6,7},{7,4},{8,9},{9,10},{10,1... | collective-permute-start | bytes 2949128 | tf_op jit(solution)/shard_map/ppermute | solution.py:20
  65.5 25.9 %copy-start.48 = (bf16[768,3,192]{0,2,1:T(8,128)(2,1)S(1)}, bf16[768,3,192]{0,2,1:T(8,128)(2,1)}, u32[]{:S(2)}) copy-start(bf16[768,3,192]{0,2,1:T(8,128)(2,1)} %param.19) | copy-start | bytes 2654212
  102.5 8.8 copy-start.8
  116.6 6.3 copy-start.1
  116.6 3.3 copy-start.10
  119.9 3.0 copy-start.28
  122.9 5.8 copy-start.27
  128.7 4.3 copy-start.11
  133.0 134.2 %copy-start.40 = (f32[768]{0:T(1024)S(1)}, f32[768]{0:T(1024)}, u32[]{:S(2)}) copy-start(f32[768]{0:T(1024)} %param.22) | copy-start | bytes 9220
  133.1 136.6 %copy-start.38 = (f32[768]{0:T(1024)S(1)}, f32[768]{0:T(1024)}, u32[]{:S(2)}) copy-start(f32[768]{0:T(1024)} %param.23) | copy-start | bytes 9220
  133.1 136.6 %copy-start.41 = (f32[768]{0:T(1024)S(1)}, f32[768]{0:T(1024)}, u32[]{:S(2)}) copy-start(f32[768]{0:T(1024)} %param.24) | copy-start | bytes 9220
  133.1 215.1 %all-gather.4.cloned.1.call-start = ((), (), s32[]{:S(2)}) async-start(), calls=%async_computation.5 | async-start | bytes 4915200 | tf_op jit(solution)/shard_map/all_gather | solution.py:195
  269.3 2.5 copy-start.44
  271.0 153.7 %all-gather.6.cloned.1.call-start = ((), (), s32[]{:S(2)}) async-start(), calls=%async_computation.7 | async-start | bytes 4915200 | tf_op jit(solution)/shard_map/all_gather | solution.py:208
  271.8 319.0 %reduce-scatter.9.cloned.1.call-start = ((), (), s32[]{:S(2)}) async-start(), calls=%async_computation.8 | async-start | bytes 9830400 | tf_op jit(solution)/shard_map/reduce_scatter | solution.py:212
  424.8 25.6 %copy-start.47 = (bf16[768,768]{1,0:T(8,128)(2,1)S(1)}, bf16[768,768]{1,0:T(8,128)(2,1)}, u32[]{:S(2)}) copy-start(bf16[768,768]{1,0:T(8,128)(2,1)} %param.25) | copy-start | bytes 3538948
  448.5 1.9 copy-start.50
  455.8 210.3 %reduce-scatter.7.cloned.1.call-start = ((), (), s32[]{:S(2)}) async-start(), calls=%async_computation.6 | async-start | bytes 4915200 | tf_op jit(solution)/shard_map/reduce_scatter | solution.py:200
  464.3 2.0 copy-start.16
  470.9 195.2 %copy-start.42 = (f32[768]{0:T(1024)S(1)}, f32[768]{0:T(1024)}, u32[]{:S(2)}) copy-start(f32[768]{0:T(1024)} %param.28) | copy-start | bytes 9220
  470.9 278.3 %all-gather.8.cloned.1.call-start = ((), (), s32[]{:S(2)}) async-start(), calls=%async_computation.9 | async-start | bytes 4915200 | tf_op jit(solution)/shard_map/all_gather | solution.py:222
  666.1 5.0 copy-start.13
  669.8 1.3 copy-start.6
  669.8 2.6 copy-start.29
  672.3 201.9 %reduce-scatter.11.cloned.1.call-start = ((), (), s32[]{:S(2)}) async-start(), calls=%async_computation.10 | async-start | bytes 4915200 | tf_op jit(solution)/shard_map/reduce_scatter | solution.py:236
  757.0 7.2 copy-start.2
  767.2 1.9 copy-start.5
  769.1 4.0 copy-start.9
  793.7 2.7 copy-start.21
  793.7 4.3 copy-start.49
  796.4 1.6 copy-start.25
  802.8 190.8 %all-reduce.5.cloned.1.call-start = ((), (), s32[]{:S(2)}) async-start(), calls=%async_computation.11 | async-start | bytes 14155776 | tf_op jit(solution)/shard_map/psum | solution.py:262
  803.1 8.2 copy-start.17
  803.1 8.2 copy-start.46
  811.3 4.9 copy-start.12
  811.3 4.9 copy-start.18
  811.3 6.6 copy-start.26
  816.1 2.4 copy-start.20
  822.2 52.0 %copy-start.4 = (bf16[640,768]{1,0:T(8,128)(2,1)S(1)}, bf16[640,768]{1,0:T(8,128)(2,1)}, u32[]{:S(2)}) copy-start(bf16[640,768]{1,0:T(8,128)(2,1)} %param.15) | copy-start | bytes 2949124
  822.2 52.0 %copy-start.31 = (f32[640]{0:T(1024)S(1)}, f32[640]{0:T(1024)}, u32[]{:S(2)}) copy-start(f32[640]{0:T(1024)} %copy-done.30) | copy-start | bytes 7684
  822.2 52.0 %copy-start.33 = (f32[768]{0:T(1024)S(1)}, f32[768]{0:T(1024)}, u32[]{:S(2)}) copy-start(f32[768]{0:T(1024)} %param.17) | copy-start | bytes 9220
  824.5 51.8 %copy-start.37 = (f32[640]{0:T(1024)S(1)}, f32[640]{0:T(1024)}, u32[]{:S(2)}) copy-start(f32[640]{0:T(1024)} %copy-done.36) | copy-start | bytes 7684
  824.5 51.8 %copy-start.35 = (f32[640]{0:T(1024)S(1)}, f32[640]{0:T(1024)}, u32[]{:S(2)}) copy-start(f32[640]{0:T(1024)} %copy-done.34) | copy-start | bytes 7684
  824.6 54.1 %copy-start.14 = (bf16[640,768]{1,0:T(8,128)(2,1)S(1)}, bf16[640,768]{1,0:T(8,128)(2,1)}, u32[]{:S(2)}) copy-start(bf16[640,768]{1,0:T(8,128)(2,1)} %param.29) | copy-start | bytes 2949124
  874.2 4.5 copy-start.7
  874.2 4.5 copy-start.15
  993.6 3.0 copy-start.24
  993.6 3.8 copy-start.23
  996.5 2.2 copy-start.22
Sparse Core Ops, SparseCore 0:
  133.2 133.9 reduce-scatter.4
  271.2 76.9 all-gather.3
  349.7 74.9 all-gather.5
  455.9 134.8 reduce-scatter.8
  592.9 73.1 reduce-scatter.6
  672.5 76.7 all-gather.7
  802.9 71.2 reduce-scatter.10
  879.0 114.5 all-reduce.4
